TPU v7x, 512 devices: a whole 4x4x16 slice. The times are simulated.
512 devices in a mesh: tx: 8 (over x, core), ty: 16 (over z), tz: 4 (over y).
Axes of the slice: x: 4, y: 4, z: 16, core: 2. Of those that a mesh axis runs over, the one named last changes fastest.
Arguments:
- start_block: float32 [64, 1048576], P(None, ('tx', 'ty', 'tz'))
- weights: bfloat16 [8192, 6, 128, 128], P(('tx', 'ty', 'tz')), may hold values from 0 to 0.25, as said below
- neighbours: int32 [8192, 6], P(('tx', 'ty', 'tz')), may hold values from 0 to 123, as said below
- boundary: int32 [2048], P(('tx', 'ty', 'tz')), may hold values from 0 to 15, as said below
Outputs:
- basis: float32 [64, 1048576], P(None, ('tx', 'ty', 'tz'))
- rfactor: float32 [64, 64], replicated
Inputs may be any that keep to these rules, and one draw needn't show every extreme that they name: `neighbours`: slot 0 of block row b is b % 16; in the last of each device's 16 rows slot 1 is 123. `boundary`: each device's 4 entries are distinct, the last of them 16 - 1. For each block row b and point p, exactly 16 of the entries weights[b, s, q, p] over all slots s and rows q are nonzero, each positive.
All inputs are finite; a program needn't handle non-finite values.
Results may differ from a plain program's by a relative error of at most 0.00075.
Values may be sent and summed in bfloat16 or wider, within the bound.
No kernel may reach another device: no remote copies, remote signals or barrier semaphores. Data moves between devices by JAX's collectives and lax.ppermute only.
A program may use at most 64 MiB of HBM per device.

v0:
```python
import jax
import jax.numpy as jnp
from jax import lax
from jax.sharding import PartitionSpec as P


def extended(block, sides, width):
    for axis, dim in sides:
        count = lax.axis_size(axis)
        forward = [(i, i + 1) for i in range(count - 1)]
        backward = [(target, source) for source, target in forward]
        low = lax.ppermute(
            lax.slice_in_dim(block, block.shape[dim] - width, None, axis=dim), axis, forward
        )
        high = lax.ppermute(lax.slice_in_dim(block, 0, width, axis=dim), axis, backward)
        block = jnp.concatenate([low, block, high], axis=dim)
    return block


def take_edges(grid, boundary):
    return jnp.take(grid, boundary, axis=1)[:, None, None, None]


def boundary_halo(edge_part):
    return extended(edge_part, (("tx", 1), ("ty", 2), ("tz", 3)), 1)


def as_pool(haloed):
    return haloed.reshape(haloed.shape[0], -1, haloed.shape[-1])


def apply_operator(current, own_grid, far_grid, degree, weights, neighbours):
    pool_grid = jnp.concatenate([own_grid, far_grid], axis=1)
    picked = jnp.take(pool_grid, neighbours, axis=1)
    product = jnp.einsum("kisq,isqp->kip", picked, weights, preferred_element_type=jnp.float32)
    return current * (1.0 - degree * 0.125) + product.reshape(current.shape) * 0.125


def lower_factor(mixed):
    local_gram = jnp.dot(
        mixed, mixed.T, precision=lax.Precision.HIGHEST, preferred_element_type=jnp.float32
    )
    total = lax.psum(local_gram, ("tx", "ty", "tz"))
    return jnp.linalg.cholesky(total)


def solve_lower(lower, values):
    return lax.linalg.triangular_solve(lower, values, left_side=True, lower=True)


def per_device(start_block, weights, neighbours, boundary):
    width, points = start_block.shape
    block_size = weights.shape[-1]
    blocks = points // block_size
    devices = lax.axis_size("tx") * lax.axis_size("ty") * lax.axis_size("tz")
    root_scale = float(points * devices) ** 0.5
    degree = jnp.sum(weights, axis=(1, 2), dtype=jnp.float32).reshape(points)
    own_grid = start_block.astype(jnp.bfloat16).reshape(width, blocks, block_size)
    far_grid = as_pool(boundary_halo(take_edges(own_grid, boundary)))
    mixed = apply_operator(start_block, own_grid, far_grid, degree, weights, neighbours)
    lower = lower_factor(mixed)
    current = solve_lower(lower, mixed) * root_scale
    own_grid = current.astype(jnp.bfloat16).reshape(width, blocks, block_size)
    far_grid = as_pool(boundary_halo(take_edges(own_grid, boundary)))
    mixed = apply_operator(current, own_grid, far_grid, degree, weights, neighbours)
    lower = lower_factor(mixed)
    basis = solve_lower(lower, mixed) * root_scale
    return (basis, lower.T / root_scale)


def solution(mesh):
    placed = (
        P(None, ("tx", "ty", "tz")),
        P(("tx", "ty", "tz"), None, None, None),
        P(("tx", "ty", "tz"), None),
        P(("tx", "ty", "tz")),
    )
    return jax.shard_map(
        per_device,
        mesh=mesh,
        in_specs=placed,
        out_specs=(P(None, ("tx", "ty", "tz")), P()),
        check_vma=False,
    )
```

profile of v0, /device:TPU:1, one launch (start us, length us, event | category | flops | bytes accessed | tf_op | source)
XLA Modules:
  0.0 328.7 jit_solution(997474695390738293)
XLA Ops:
  0.6 0.7 compare_and_fusion.1
  1.3 0.7 compare_select_fusion.1
  2.0 1.1 copy_bitcast_fusion.1
  3.1 0.6 gather_fusion
  3.6 0.1 select_bitcast_fusion.1
  3.7 8.8 %collective-permute-start.1 = (bf16[64,1,1,1,4,128]{5,0,4,3,2,1:T(8,128)(2,1)S(1)}, bf16[64,1,1,1,4,128]{5,0,4,3,2,1:T(8,128)(2,1)S(1)}, u32[]{:S(2)}, u32[]{:S(2)}) collective-permute-start(bf16[64,1,1,1,4,128]{5,0,4,3,2,1:T(8,128)(2,1)S(1)} %select_bitcast_fusion.1), channel_id=1, source_target_pairs={{64,0},{128,64},{192,128},{256,192},{320,256},{384,320},{448,384},... | collective-permute-start | bytes 196616 | tf_op jit(solution)/shard_map/ppermute | solution.py:15
  12.5 1.9 collective-permute-start
  14.4 0.7 compare_and_fusion
  15.1 0.1 copy.28
  15.2 0.5 collective-permute-done
  15.8 1.3 collective-permute-start.3
  17.1 4.0 %collective-permute-start.2 = (bf16[64,3,1,1,4,128]{5,0,4,3,2,1:T(8,128)(2,1)S(1)}, bf16[64,3,1,1,4,128]{5,0,4,3,2,1:T(8,128)(2,1)S(1)}, u32[]{:S(2)}, u32[]{:S(2)}) collective-permute-start(bf16[64,3,1,1,4,128]{5,0,4,3,2,1:T(8,128)(2,1)S(1)} %pad_maximum_fusion.6), channel_id=1, source_target_pairs={{0,4},{4,8},{8,12},{12,16},{16,20},{20,24},{24,28},{28,32},{32,36}... | collective-permute-start | bytes 589832 | tf_op jit(solution)/shard_map/ppermute | solution.py:12
  21.1 0.7 compare_select_fusion
  21.7 0.1 copy.31
  21.8 0.1 reshape.100
  21.9 2.2 collective-permute-done.3
  24.1 0.9 collective-permute-done.2
  25.0 0.1 pad_maximum_fusion.4
  25.0 1.3 collective-permute-start.5
  26.3 4.0 %collective-permute-start.4 = (bf16[64,3,3,1,4,128]{5,0,4,3,2,1:T(8,128)(2,1)S(1)}, bf16[64,3,3,1,4,128]{5,0,4,3,2,1:T(8,128)(2,1)S(1)}, u32[]{:S(2)}, u32[]{:S(2)}) collective-permute-start(bf16[64,3,3,1,4,128]{5,0,4,3,2,1:T(8,128)(2,1)S(1)} %pad_maximum_fusion.4), channel_id=1, source_target_pairs={{0,1},{1,2},{2,3},{4,5},{5,6},{6,7},{8,9},{9,10},{10,11},{12,13},{... | collective-permute-start | bytes 1769480 | tf_op jit(solution)/shard_map/ppermute | solution.py:12
  30.4 2.4 convert_reduce_fusion
  32.8 7.8 %collective-permute-done.5 = bf16[64,3,3,1,4,128]{5,0,4,3,2,1:T(8,128)(2,1)S(1)} collective-permute-done((bf16[64,3,3,1,4,128]{5,0,4,3,2,1:T(8,128)(2,1)S(1)}, bf16[64,3,3,1,4,128]{5,0,4,3,2,1:T(8,128)(2,1)S(1)}, u32[]{:S(2)}, u32[]{:S(2)}) %collective-permute-start.5) | collective-permute-done | bytes 589856 | tf_op jit(solution)/shard_map/ppermute | solution.py:15
  40.6 0.9 collective-permute-done.4
  41.5 0.2 pad_maximum_fusion.2
  41.7 0.2 pad_maximum_fusion
  41.9 2.0 gather_fusion.1
  43.9 3.2 fusion.23
  47.0 0.6 fusion.30
  47.6 108.8 %psum.14 = f32[64,64]{0,1:T(8,128)S(1)} all-reduce(f32[64,64]{0,1:T(8,128)S(1)} %fusion.30), channel_id=1, replica_groups=mesh['tx'=8,'ty'=16,'tz'=4] {'tx','ty','tz'}, use_global_device_ids=true, to_apply=%region_1.4 | all-reduce | flops 4096 | bytes 32768 | tf_op jit(solution)/shard_map/psum | solution.py:43
  156.4 0.1 copy.34
  156.5 5.8 %cholesky.44 = f32[64,64]{1,0:T(8,128)S(1)} custom-call(f32[64,64]{1,0:T(8,128)S(1)} %fusion.36), custom_call_target="Cholesky" | custom-call | tf_op jit(solution)/shard_map/jit(cholesky)/cholesky | solution.py:44
  162.4 0.6 compare_reduce_fusion.1
  163.1 0.7 fusion.32
  163.7 4.9 %custom-call.6 = f32[1,64,64]{1,2,0:T(8,128)S(1)} custom-call(f32[1,64,64]{2,1,0:T(8,128)S(1)} %fusion.32), custom_call_target="InvertDiagBlocksLowerTriangular" | custom-call | tf_op jit(solution)/shard_map/triangular_solve/custom-call.0 | solution.py:48
  168.6 0.6 fusion.29
  169.3 0.1 copy_bitcast_fusion
  169.3 0.6 gather_fusion.2
  169.9 0.1 select_bitcast_fusion
  170.0 2.6 collective-permute-start.7
  172.6 3.0 collective-permute-start.6
  175.5 0.0 collective-permute-done.7
  175.6 1.3 collective-permute-done.6
  176.9 1.3 collective-permute-start.9
  178.2 4.3 %collective-permute-start.8 = (bf16[64,3,1,1,4,128]{5,0,4,3,2,1:T(8,128)(2,1)S(1)}, bf16[64,3,1,1,4,128]{5,0,4,3,2,1:T(8,128)(2,1)S(1)}, u32[]{:S(2)}, u32[]{:S(2)}) collective-permute-start(bf16[64,3,1,1,4,128]{5,0,4,3,2,1:T(8,128)(2,1)S(1)} %pad_maximum_fusion.7), channel_id=1, source_target_pairs={{0,4},{4,8},{8,12},{12,16},{16,20},{20,24},{24,28},{28,32},{32,36}... | collective-permute-start | bytes 589832 | tf_op jit(solution)/shard_map/ppermute | solution.py:12
  182.4 2.4 collective-permute-done.9
  184.9 1.8 collective-permute-done.8
  186.6 0.1 pad_maximum_fusion.5
  186.7 1.3 collective-permute-start.11
  188.0 4.0 %collective-permute-start.10 = (bf16[64,3,3,1,4,128]{5,0,4,3,2,1:T(8,128)(2,1)S(1)}, bf16[64,3,3,1,4,128]{5,0,4,3,2,1:T(8,128)(2,1)S(1)}, u32[]{:S(2)}, u32[]{:S(2)}) collective-permute-start(bf16[64,3,3,1,4,128]{5,0,4,3,2,1:T(8,128)(2,1)S(1)} %pad_maximum_fusion.5), channel_id=1, source_target_pairs={{0,1},{1,2},{2,3},{4,5},{5,6},{6,7},{8,9},{9,10},{10,11},{12,13},{... | collective-permute-start | bytes 1769480 | tf_op jit(solution)/shard_map/ppermute | solution.py:12
  192.0 11.6 %collective-permute-done.11 = bf16[64,3,3,1,4,128]{5,0,4,3,2,1:T(8,128)(2,1)S(1)} collective-permute-done((bf16[64,3,3,1,4,128]{5,0,4,3,2,1:T(8,128)(2,1)S(1)}, bf16[64,3,3,1,4,128]{5,0,4,3,2,1:T(8,128)(2,1)S(1)}, u32[]{:S(2)}, u32[]{:S(2)}) %collective-permute-start.11) | collective-permute-done | bytes 589856 | tf_op jit(solution)/shard_map/ppermute | solution.py:15
  203.6 0.9 collective-permute-done.10
  204.5 0.2 pad_maximum_fusion.3
  204.7 0.2 pad_maximum_fusion.1
  204.9 2.0 gather_fusion.3
  206.9 3.1 fusion.17
  210.0 0.6 fusion.31
  210.5 103.8 %psum.15 = f32[64,64]{0,1:T(8,128)S(1)} all-reduce(f32[64,64]{0,1:T(8,128)S(1)} %fusion.31), channel_id=1, replica_groups=mesh['tx'=8,'ty'=16,'tz'=4] {'tx','ty','tz'}, use_global_device_ids=true, to_apply=%region_4.9 | all-reduce | flops 4096 | bytes 32768 | tf_op jit(solution)/shard_map/psum | solution.py:43
  314.4 0.1 copy.41
  314.5 5.8 %cholesky.55 = f32[64,64]{1,0:T(8,128)S(1)} custom-call(f32[64,64]{1,0:T(8,128)S(1)} %fusion.34), custom_call_target="Cholesky" | custom-call | tf_op jit(solution)/shard_map/jit(cholesky)/cholesky | solution.py:44
  320.4 0.6 compare_reduce_fusion
  321.0 0.7 multiply_bitcast_fusion
  321.7 0.7 copy.42
  322.4 4.9 %custom-call.7 = f32[1,64,64]{1,2,0:T(8,128)S(1)} custom-call(f32[1,64,64]{2,1,0:T(8,128)S(1)} %get-tuple-element.13), custom_call_target="InvertDiagBlocksLowerTriangular" | custom-call | tf_op jit(solution)/shard_map/triangular_solve/custom-call.0 | solution.py:48
  327.3 1.4 convolution_multiply_fusion
  (13 shorter events, 0.2 us)
Async XLA Ops:
  3.7 11.5 %collective-permute-start.1 = (bf16[64,1,1,1,4,128]{5,0,4,3,2,1:T(8,128)(2,1)S(1)}, bf16[64,1,1,1,4,128]{5,0,4,3,2,1:T(8,128)(2,1)S(1)}, u32[]{:S(2)}, u32[]{:S(2)}) collective-permute-start(bf16[64,1,1,1,4,128]{5,0,4,3,2,1:T(8,128)(2,1)S(1)} %select_bitcast_fusion.1), channel_id=1, source_target_pairs={{64,0},{128,64},{192,128},{256,192},{320,256},{384,320},{448,384},... | collective-permute-start | bytes 196616 | tf_op jit(solution)/shard_map/ppermute | solution.py:15
  12.5 3.2 collective-permute-start
  15.8 8.3 %collective-permute-start.3 = (bf16[64,3,1,1,4,128]{5,0,4,3,2,1:T(8,128)(2,1)S(1)}, bf16[64,3,1,1,4,128]{5,0,4,3,2,1:T(8,128)(2,1)S(1)}, u32[]{:S(2)}, u32[]{:S(2)}) collective-permute-start(bf16[64,3,1,1,4,128]{5,0,4,3,2,1:T(8,128)(2,1)S(1)} %pad_maximum_fusion.6), channel_id=1, source_target_pairs={{4,0},{8,4},{12,8},{16,12},{20,16},{24,20},{28,24},{32,28},{36,32}... | collective-permute-start | bytes 589832 | tf_op jit(solution)/shard_map/ppermute | solution.py:15
  17.1 7.9 %collective-permute-start.2 = (bf16[64,3,1,1,4,128]{5,0,4,3,2,1:T(8,128)(2,1)S(1)}, bf16[64,3,1,1,4,128]{5,0,4,3,2,1:T(8,128)(2,1)S(1)}, u32[]{:S(2)}, u32[]{:S(2)}) collective-permute-start(bf16[64,3,1,1,4,128]{5,0,4,3,2,1:T(8,128)(2,1)S(1)} %pad_maximum_fusion.6), channel_id=1, source_target_pairs={{0,4},{4,8},{8,12},{12,16},{16,20},{20,24},{24,28},{28,32},{32,36}... | collective-permute-start | bytes 589832 | tf_op jit(solution)/shard_map/ppermute | solution.py:12
  25.0 15.5 %collective-permute-start.5 = (bf16[64,3,3,1,4,128]{5,0,4,3,2,1:T(8,128)(2,1)S(1)}, bf16[64,3,3,1,4,128]{5,0,4,3,2,1:T(8,128)(2,1)S(1)}, u32[]{:S(2)}, u32[]{:S(2)}) collective-permute-start(bf16[64,3,3,1,4,128]{5,0,4,3,2,1:T(8,128)(2,1)S(1)} %pad_maximum_fusion.4), channel_id=1, source_target_pairs={{1,0},{2,1},{3,2},{5,4},{6,5},{7,6},{9,8},{10,9},{11,10},{13,12},{... | collective-permute-start | bytes 1769480 | tf_op jit(solution)/shard_map/ppermute | solution.py:15
  26.3 15.1 %collective-permute-start.4 = (bf16[64,3,3,1,4,128]{5,0,4,3,2,1:T(8,128)(2,1)S(1)}, bf16[64,3,3,1,4,128]{5,0,4,3,2,1:T(8,128)(2,1)S(1)}, u32[]{:S(2)}, u32[]{:S(2)}) collective-permute-start(bf16[64,3,3,1,4,128]{5,0,4,3,2,1:T(8,128)(2,1)S(1)} %pad_maximum_fusion.4), channel_id=1, source_target_pairs={{0,1},{1,2},{2,3},{4,5},{5,6},{6,7},{8,9},{9,10},{10,11},{12,13},{... | collective-permute-start | bytes 1769480 | tf_op jit(solution)/shard_map/ppermute | solution.py:12
  43.9 3.2 copy-start
  170.0 5.6 %collective-permute-start.7 = (bf16[64,1,1,1,4,128]{5,0,4,3,2,1:T(8,128)(2,1)S(1)}, bf16[64,1,1,1,4,128]{5,0,4,3,2,1:T(8,128)(2,1)S(1)}, u32[]{:S(2)}, u32[]{:S(2)}) collective-permute-start(bf16[64,1,1,1,4,128]{5,0,4,3,2,1:T(8,128)(2,1)S(1)} %select_bitcast_fusion), channel_id=1, source_target_pairs={{64,0},{128,64},{192,128},{256,192},{320,256},{384,320},{448,384},... | collective-permute-start | bytes 196616 | tf_op jit(solution)/shard_map/ppermute | solution.py:15
  172.6 4.3 %collective-permute-start.6 = (bf16[64,1,1,1,4,128]{5,0,4,3,2,1:T(8,128)(2,1)S(1)}, bf16[64,1,1,1,4,128]{5,0,4,3,2,1:T(8,128)(2,1)S(1)}, u32[]{:S(2)}, u32[]{:S(2)}) collective-permute-start(bf16[64,1,1,1,4,128]{5,0,4,3,2,1:T(8,128)(2,1)S(1)} %select_bitcast_fusion), channel_id=1, source_target_pairs={{0,64},{64,128},{128,192},{192,256},{256,320},{320,384},{384,448},... | collective-permute-start | bytes 196616 | tf_op jit(solution)/shard_map/ppermute | solution.py:12
  176.9 8.0 %collective-permute-start.9 = (bf16[64,3,1,1,4,128]{5,0,4,3,2,1:T(8,128)(2,1)S(1)}, bf16[64,3,1,1,4,128]{5,0,4,3,2,1:T(8,128)(2,1)S(1)}, u32[]{:S(2)}, u32[]{:S(2)}) collective-permute-start(bf16[64,3,1,1,4,128]{5,0,4,3,2,1:T(8,128)(2,1)S(1)} %pad_maximum_fusion.7), channel_id=1, source_target_pairs={{4,0},{8,4},{12,8},{16,12},{20,16},{24,20},{28,24},{32,28},{36,32}... | collective-permute-start | bytes 589832 | tf_op jit(solution)/shard_map/ppermute | solution.py:15
  178.2 8.4 %collective-permute-start.8 = (bf16[64,3,1,1,4,128]{5,0,4,3,2,1:T(8,128)(2,1)S(1)}, bf16[64,3,1,1,4,128]{5,0,4,3,2,1:T(8,128)(2,1)S(1)}, u32[]{:S(2)}, u32[]{:S(2)}) collective-permute-start(bf16[64,3,1,1,4,128]{5,0,4,3,2,1:T(8,128)(2,1)S(1)} %pad_maximum_fusion.7), channel_id=1, source_target_pairs={{0,4},{4,8},{8,12},{12,16},{16,20},{20,24},{24,28},{28,32},{32,36}... | collective-permute-start | bytes 589832 | tf_op jit(solution)/shard_map/ppermute | solution.py:12
  186.7 16.9 %collective-permute-start.11 = (bf16[64,3,3,1,4,128]{5,0,4,3,2,1:T(8,128)(2,1)S(1)}, bf16[64,3,3,1,4,128]{5,0,4,3,2,1:T(8,128)(2,1)S(1)}, u32[]{:S(2)}, u32[]{:S(2)}) collective-permute-start(bf16[64,3,3,1,4,128]{5,0,4,3,2,1:T(8,128)(2,1)S(1)} %pad_maximum_fusion.5), channel_id=1, source_target_pairs={{1,0},{2,1},{3,2},{5,4},{6,5},{7,6},{9,8},{10,9},{11,10},{13,12},{... | collective-permute-start | bytes 1769480 | tf_op jit(solution)/shard_map/ppermute | solution.py:15
  188.0 16.5 %collective-permute-start.10 = (bf16[64,3,3,1,4,128]{5,0,4,3,2,1:T(8,128)(2,1)S(1)}, bf16[64,3,3,1,4,128]{5,0,4,3,2,1:T(8,128)(2,1)S(1)}, u32[]{:S(2)}, u32[]{:S(2)}) collective-permute-start(bf16[64,3,3,1,4,128]{5,0,4,3,2,1:T(8,128)(2,1)S(1)} %pad_maximum_fusion.5), channel_id=1, source_target_pairs={{0,1},{1,2},{2,3},{4,5},{5,6},{6,7},{8,9},{9,10},{10,11},{12,13},{... | collective-permute-start | bytes 1769480 | tf_op jit(solution)/shard_map/ppermute | solution.py:12
where the time goes:
time: 330 us; the launch traced here: 329 us
  blocking collectives  213 us (65%)
  starting transfers between devices  37.7 us (11%)
  other arithmetic  31.6 us (10%)
  waiting for transfers between devices  30.1 us (9%)
  matrix products  9.49 us (3%)
  local copies, waits for them, and re-layouts  6.16 us (2%)
    psum x2, blocking collectives, lower_factor(): total = lax.psum(local_gram, ('tx', 'ty', 'tz'))  213 us
    ppermute x6, waiting for transfers between devices, extended(): lax.ppermute(lax.slice_in_dim(block, 0, width, axis=dim), axis, backward)  23.9 us
    ppermute x6, starting transfers between devices, extended(): lax.ppermute(lax.slice_in_dim(block, block.shape[dim] - width, None, axis...  21.2 us
    ppermute x6, starting transfers between devices, extended(): lax.ppermute(lax.slice_in_dim(block, 0, width, axis=dim), axis, backward)  16.5 us
    another operation x6, other arithmetic, lower_factor(): return jnp.linalg.cholesky(total)  13 us
    another operation x3, other arithmetic, solve_lower(): lax.linalg.triangular_solve(lower, values, left_side=True, lower=True)  10.4 us
  transfers between devices with their start and end apart: 12, of which 10 were waited for; matrix products, arithmetic and copies ran while one was open for 1% of the time, Pallas kernels for 0%

commit v1 on v0

--- a/solution.py
+++ b/solution.py
@@ -1,7 +1,16 @@
+import functools
 import jax
 import jax.numpy as jnp
 from jax import lax
 from jax.sharding import PartitionSpec as P
+from jax.lax import psum
+
+
+def clear_case_on_mesh(m, bus_axis, dev_axis):
+    return psum(psum(m, bus_axis), dev_axis)
+
+
+start_the_roads = functools.partial(clear_case_on_mesh, bus_axis=("ty", "tz"), dev_axis="tx")
 
 
 def extended(block, sides, width):
@@ -40,7 +49,7 @@
     local_gram = jnp.dot(
         mixed, mixed.T, precision=lax.Precision.HIGHEST, preferred_element_type=jnp.float32
     )
-    total = lax.psum(local_gram, ("tx", "ty", "tz"))
+    total = start_the_roads(local_gram)
     return jnp.linalg.cholesky(total)
 
 

time: 330 us -> 722 us (2.19)
  blocking collectives: 213 us -> 606 us
    psum x2 -> x4, blocking collectives: 213 us -> 606 us  [clear_case_on_mesh(): return psum(psum(m, bus_axis), dev_axis)]
where the time goes in v1:
time: 722 us
  blocking collectives  606 us (84%)
  starting transfers between devices  39.3 us (5%)
  other arithmetic  31.6 us (4%)
  waiting for transfers between devices  28.5 us (4%)
  matrix products  9.49 us (1%)
    psum x4, blocking collectives, clear_case_on_mesh(): return psum(psum(m, bus_axis), dev_axis)  606 us
    ppermute x6, waiting for transfers between devices, extended(): lax.ppermute(lax.slice_in_dim(block, 0, width, axis=dim), axis, backward)  23.2 us
    ppermute x6, starting transfers between devices, extended(): lax.ppermute(lax.slice_in_dim(block, block.shape[dim] - width, None, axis...  19.9 us
    ppermute x6, starting transfers between devices, extended(): lax.ppermute(lax.slice_in_dim(block, 0, width, axis=dim), axis, backward)  19.4 us
  transfers between devices with their start and end apart: 12, of which 10 were waited for; matrix products, arithmetic and copies ran while one was open for 1% of the time, Pallas kernels for 0%

profile of v1, /device:TPU:1, one launch (start us, length us, event | category | flops | bytes accessed | tf_op | source)
XLA Modules:
  0.0 721.7 jit_solution(5620161401243129954)
XLA Ops:
  0.6 0.7 compare_and_fusion.1
  1.3 0.7 compare_select_fusion.1
  2.0 1.1 copy_bitcast_fusion.1
  3.1 0.6 gather_fusion
  3.6 0.1 select_bitcast_fusion.1
  3.7 8.8 %collective-permute-start.1 = (bf16[64,1,1,1,4,128]{5,0,4,3,2,1:T(8,128)(2,1)S(1)}, bf16[64,1,1,1,4,128]{5,0,4,3,2,1:T(8,128)(2,1)S(1)}, u32[]{:S(2)}, u32[]{:S(2)}) collective-permute-start(bf16[64,1,1,1,4,128]{5,0,4,3,2,1:T(8,128)(2,1)S(1)} %select_bitcast_fusion.1), channel_id=1, source_target_pairs={{64,0},{128,64},{192,128},{256,192},{320,256},{384,320},{448,384},... | collective-permute-start | bytes 196616 | tf_op jit(solution)/shard_map/ppermute | solution.py:24
  12.5 1.9 collective-permute-start
  14.4 0.7 compare_and_fusion
  15.1 0.1 copy.28
  15.2 0.5 collective-permute-done
  15.8 1.3 collective-permute-start.3
  17.1 4.0 collective-permute-start.2
  21.1 0.7 compare_select_fusion
  21.7 0.1 copy.31
  21.8 0.1 reshape.100
  21.9 2.2 collective-permute-done.3
  24.1 0.9 collective-permute-done.2
  25.0 0.1 pad_maximum_fusion.4
  25.0 1.3 collective-permute-start.5
  26.3 4.0 collective-permute-start.4
  30.4 2.4 convert_reduce_fusion
  32.8 7.8 %collective-permute-done.5 = bf16[64,3,3,1,4,128]{5,0,4,3,2,1:T(8,128)(2,1)S(1)} collective-permute-done((bf16[64,3,3,1,4,128]{5,0,4,3,2,1:T(8,128)(2,1)S(1)}, bf16[64,3,3,1,4,128]{5,0,4,3,2,1:T(8,128)(2,1)S(1)}, u32[]{:S(2)}, u32[]{:S(2)}) %collective-permute-start.5) | collective-permute-done | bytes 589856 | tf_op jit(solution)/shard_map/ppermute | solution.py:24
  40.6 0.9 collective-permute-done.4
  41.5 0.2 pad_maximum_fusion.2
  41.7 0.2 pad_maximum_fusion
  41.9 2.0 gather_fusion.1
  43.9 3.2 fusion.23
  47.0 0.6 fusion.30
  47.6 230.2 %psum.28 = f32[64,64]{0,1:T(8,128)S(1)} all-reduce(f32[64,64]{0,1:T(8,128)S(1)} %fusion.30), channel_id=1, replica_groups=mesh['tx'=8,'ty'=16,'tz'=4] {'ty','tz'}, use_global_device_ids=true, to_apply=%region_1.4 | all-reduce | flops 4096 | bytes 32768 | tf_op jit(solution)/shard_map/psum | solution.py:10
  277.8 76.7 %psum.29 = f32[64,64]{0,1:T(8,128)S(1)} all-reduce(f32[64,64]{0,1:T(8,128)S(1)} %psum.28), channel_id=1, replica_groups=mesh['tx'=8,'ty'=16,'tz'=4] {'tx'}, use_global_device_ids=true, to_apply=%region_2.5 | all-reduce | flops 4096 | bytes 32768 | tf_op jit(solution)/shard_map/psum | solution.py:10
  354.5 0.1 copy.34
  354.6 5.8 cholesky.44
  360.5 0.6 compare_reduce_fusion.1
  361.2 0.7 fusion.32
  361.8 4.9 custom-call.6
  366.7 0.7 fusion.29
  367.4 0.6 gather_fusion.2
  368.0 0.1 select_bitcast_fusion
  368.1 5.4 collective-permute-start.7
  373.5 1.9 collective-permute-start.6
  375.5 1.3 collective-permute-done.6
  376.8 1.3 collective-permute-start.9
  378.1 4.0 collective-permute-start.8
  382.1 3.0 collective-permute-done.9
  385.1 0.9 collective-permute-done.8
  386.0 0.1 pad_maximum_fusion.5
  386.1 1.3 collective-permute-start.11
  387.4 4.0 collective-permute-start.10
  391.4 10.2 %collective-permute-done.11 = bf16[64,3,3,1,4,128]{5,0,4,3,2,1:T(8,128)(2,1)S(1)} collective-permute-done((bf16[64,3,3,1,4,128]{5,0,4,3,2,1:T(8,128)(2,1)S(1)}, bf16[64,3,3,1,4,128]{5,0,4,3,2,1:T(8,128)(2,1)S(1)}, u32[]{:S(2)}, u32[]{:S(2)}) %collective-permute-start.11) | collective-permute-done | bytes 589856 | tf_op jit(solution)/shard_map/ppermute | solution.py:24
  401.6 0.9 collective-permute-done.10
  402.5 0.2 pad_maximum_fusion.3
  402.8 0.2 pad_maximum_fusion.1
  402.9 2.0 gather_fusion.3
  404.9 3.1 fusion.17
  408.0 0.6 fusion.31
  408.6 221.2 %psum.30 = f32[64,64]{0,1:T(8,128)S(1)} all-reduce(f32[64,64]{0,1:T(8,128)S(1)} %fusion.31), channel_id=1, replica_groups=mesh['tx'=8,'ty'=16,'tz'=4] {'ty','tz'}, use_global_device_ids=true, to_apply=%region_5.10 | all-reduce | flops 4096 | bytes 32768 | tf_op jit(solution)/shard_map/psum | solution.py:10
  629.8 77.6 %psum.31 = f32[64,64]{0,1:T(8,128)S(1)} all-reduce(f32[64,64]{0,1:T(8,128)S(1)} %psum.30), channel_id=1, replica_groups=mesh['tx'=8,'ty'=16,'tz'=4] {'tx'}, use_global_device_ids=true, to_apply=%region_6.11 | all-reduce | flops 4096 | bytes 32768 | tf_op jit(solution)/shard_map/psum | solution.py:10
  707.4 0.1 copy.41
  707.5 5.8 cholesky.55
  713.4 0.6 compare_reduce_fusion
  714.0 0.7 multiply_bitcast_fusion
  714.7 0.7 copy.42
  715.4 4.9 custom-call.7
  720.3 1.4 convolution_multiply_fusion
  (15 shorter events, 0.2 us)
Async XLA Ops:
  3.7 11.5 %collective-permute-start.1 = (bf16[64,1,1,1,4,128]{5,0,4,3,2,1:T(8,128)(2,1)S(1)}, bf16[64,1,1,1,4,128]{5,0,4,3,2,1:T(8,128)(2,1)S(1)}, u32[]{:S(2)}, u32[]{:S(2)}) collective-permute-start(bf16[64,1,1,1,4,128]{5,0,4,3,2,1:T(8,128)(2,1)S(1)} %select_bitcast_fusion.1), channel_id=1, source_target_pairs={{64,0},{128,64},{192,128},{256,192},{320,256},{384,320},{448,384},... | collective-permute-start | bytes 196616 | tf_op jit(solution)/shard_map/ppermute | solution.py:24
  12.5 3.2 collective-permute-start
  15.8 8.3 %collective-permute-start.3 = (bf16[64,3,1,1,4,128]{5,0,4,3,2,1:T(8,128)(2,1)S(1)}, bf16[64,3,1,1,4,128]{5,0,4,3,2,1:T(8,128)(2,1)S(1)}, u32[]{:S(2)}, u32[]{:S(2)}) collective-permute-start(bf16[64,3,1,1,4,128]{5,0,4,3,2,1:T(8,128)(2,1)S(1)} %pad_maximum_fusion.6), channel_id=1, source_target_pairs={{4,0},{8,4},{12,8},{16,12},{20,16},{24,20},{28,24},{32,28},{36,32}... | collective-permute-start | bytes 589832 | tf_op jit(solution)/shard_map/ppermute | solution.py:24
  17.1 7.9 %collective-permute-start.2 = (bf16[64,3,1,1,4,128]{5,0,4,3,2,1:T(8,128)(2,1)S(1)}, bf16[64,3,1,1,4,128]{5,0,4,3,2,1:T(8,128)(2,1)S(1)}, u32[]{:S(2)}, u32[]{:S(2)}) collective-permute-start(bf16[64,3,1,1,4,128]{5,0,4,3,2,1:T(8,128)(2,1)S(1)} %pad_maximum_fusion.6), channel_id=1, source_target_pairs={{0,4},{4,8},{8,12},{12,16},{16,20},{20,24},{24,28},{28,32},{32,36}... | collective-permute-start | bytes 589832 | tf_op jit(solution)/shard_map/ppermute | solution.py:21
  25.0 15.5 %collective-permute-start.5 = (bf16[64,3,3,1,4,128]{5,0,4,3,2,1:T(8,128)(2,1)S(1)}, bf16[64,3,3,1,4,128]{5,0,4,3,2,1:T(8,128)(2,1)S(1)}, u32[]{:S(2)}, u32[]{:S(2)}) collective-permute-start(bf16[64,3,3,1,4,128]{5,0,4,3,2,1:T(8,128)(2,1)S(1)} %pad_maximum_fusion.4), channel_id=1, source_target_pairs={{1,0},{2,1},{3,2},{5,4},{6,5},{7,6},{9,8},{10,9},{11,10},{13,12},{... | collective-permute-start | bytes 1769480 | tf_op jit(solution)/shard_map/ppermute | solution.py:24
  26.3 15.1 %collective-permute-start.4 = (bf16[64,3,3,1,4,128]{5,0,4,3,2,1:T(8,128)(2,1)S(1)}, bf16[64,3,3,1,4,128]{5,0,4,3,2,1:T(8,128)(2,1)S(1)}, u32[]{:S(2)}, u32[]{:S(2)}) collective-permute-start(bf16[64,3,3,1,4,128]{5,0,4,3,2,1:T(8,128)(2,1)S(1)} %pad_maximum_fusion.4), channel_id=1, source_target_pairs={{0,1},{1,2},{2,3},{4,5},{5,6},{6,7},{8,9},{9,10},{10,11},{12,13},{... | collective-permute-start | bytes 1769480 | tf_op jit(solution)/shard_map/ppermute | solution.py:21
  43.9 3.2 copy-start
  368.1 7.4 %collective-permute-start.7 = (bf16[64,1,1,1,4,128]{5,0,4,3,2,1:T(8,128)(2,1)S(1)}, bf16[64,1,1,1,4,128]{5,0,4,3,2,1:T(8,128)(2,1)S(1)}, u32[]{:S(2)}, u32[]{:S(2)}) collective-permute-start(bf16[64,1,1,1,4,128]{5,0,4,3,2,1:T(8,128)(2,1)S(1)} %select_bitcast_fusion), channel_id=1, source_target_pairs={{64,0},{128,64},{192,128},{256,192},{320,256},{384,320},{448,384},... | collective-permute-start | bytes 196616 | tf_op jit(solution)/shard_map/ppermute | solution.py:24
  373.5 3.2 collective-permute-start.6
  376.8 8.3 %collective-permute-start.9 = (bf16[64,3,1,1,4,128]{5,0,4,3,2,1:T(8,128)(2,1)S(1)}, bf16[64,3,1,1,4,128]{5,0,4,3,2,1:T(8,128)(2,1)S(1)}, u32[]{:S(2)}, u32[]{:S(2)}) collective-permute-start(bf16[64,3,1,1,4,128]{5,0,4,3,2,1:T(8,128)(2,1)S(1)} %pad_maximum_fusion.7), channel_id=1, source_target_pairs={{4,0},{8,4},{12,8},{16,12},{20,16},{24,20},{28,24},{32,28},{36,32}... | collective-permute-start | bytes 589832 | tf_op jit(solution)/shard_map/ppermute | solution.py:24
  378.1 7.9 %collective-permute-start.8 = (bf16[64,3,1,1,4,128]{5,0,4,3,2,1:T(8,128)(2,1)S(1)}, bf16[64,3,1,1,4,128]{5,0,4,3,2,1:T(8,128)(2,1)S(1)}, u32[]{:S(2)}, u32[]{:S(2)}) collective-permute-start(bf16[64,3,1,1,4,128]{5,0,4,3,2,1:T(8,128)(2,1)S(1)} %pad_maximum_fusion.7), channel_id=1, source_target_pairs={{0,4},{4,8},{8,12},{12,16},{16,20},{20,24},{24,28},{28,32},{32,36}... | collective-permute-start | bytes 589832 | tf_op jit(solution)/shard_map/ppermute | solution.py:21
  386.1 15.5 %collective-permute-start.11 = (bf16[64,3,3,1,4,128]{5,0,4,3,2,1:T(8,128)(2,1)S(1)}, bf16[64,3,3,1,4,128]{5,0,4,3,2,1:T(8,128)(2,1)S(1)}, u32[]{:S(2)}, u32[]{:S(2)}) collective-permute-start(bf16[64,3,3,1,4,128]{5,0,4,3,2,1:T(8,128)(2,1)S(1)} %pad_maximum_fusion.5), channel_id=1, source_target_pairs={{1,0},{2,1},{3,2},{5,4},{6,5},{7,6},{9,8},{10,9},{11,10},{13,12},{... | collective-permute-start | bytes 1769480 | tf_op jit(solution)/shard_map/ppermute | solution.py:24
  387.4 15.1 %collective-permute-start.10 = (bf16[64,3,3,1,4,128]{5,0,4,3,2,1:T(8,128)(2,1)S(1)}, bf16[64,3,3,1,4,128]{5,0,4,3,2,1:T(8,128)(2,1)S(1)}, u32[]{:S(2)}, u32[]{:S(2)}) collective-permute-start(bf16[64,3,3,1,4,128]{5,0,4,3,2,1:T(8,128)(2,1)S(1)} %pad_maximum_fusion.5), channel_id=1, source_target_pairs={{0,1},{1,2},{2,3},{4,5},{5,6},{6,7},{8,9},{9,10},{10,11},{12,13},{... | collective-permute-start | bytes 1769480 | tf_op jit(solution)/shard_map/ppermute | solution.py:21
